TPU v7x, 512 devices: a whole 4x8x8 slice. The times are simulated.
512 devices in a mesh: grp: 8 (over y_lo, x), sub: 64 (over z, y_hi, core).
Axes of the slice: x: 4, y: 8 (y_hi: 4, y_lo: 2; y = y_hi * 2 + y_lo), z: 8, core: 2. Of those that a mesh axis runs over, the one named last changes fastest.
Arguments:
- schur_t: bfloat16 [8, 64, 1024, 1024], P('grp', 'sub')
- neumann_t: bfloat16 [8, 64, 1024, 1024], P('grp', 'sub')
- face_weights: float32 [8, 64, 1024], P('grp', 'sub'), as said below
- coarse_basis: bfloat16 [8, 64, 1024, 24], P('grp', 'sub'), may hold values from -0.375 to 0.375
- coarse_inverse: float32 [8, 768, 768], P('grp', 'sub')
- coarse_number: int32 [8, 1536], P('grp'), may hold values from 0 to 767, as said below
- loads: bfloat16 [8, 64, 1024, 128], P('grp', 'sub'), may hold values from -6 to 6
- iterate: bfloat16 [8, 64, 1024, 128], P('grp', 'sub'), as said below
Outputs:
- iterate_out: bfloat16 [8, 64, 1024, 128], P('grp', 'sub')
Inputs may be any that keep to these rules, and one draw needn't show every extreme that they name: `face_weights`: the weights of an unknown and of its partner unknown on the face it shares sum to one. `coarse_number`: each value appears exactly twice in each group's row. `iterate`: equal on the two copies of each shared unknown.
All inputs are finite; a program needn't handle non-finite values.
Results may differ from a plain program's by a relative error of at most 0.0051.
Values sent between devices are 32-bit elements; how exact they have to be, the bound alone decides.
A program may use at most 64 MiB of HBM per device.

v0:
```python
import jax
import jax.numpy as jnp
from jax import lax
from jax.sharding import PartitionSpec as P

ITERS = 3


def extended(array, sides, width):
    for axis, dim in sides:
        devices, length = (lax.axis_size(axis), array.shape[dim])
        up = [(i, (i + 1) % devices) for i in range(devices)]
        down = [(j, i) for i, j in up]
        last = lax.slice_in_dim(array, length - width, length, axis=dim)
        leading = lax.slice_in_dim(array, 0, width, axis=dim)
        before = lax.ppermute(last, axis, up)
        after = lax.ppermute(leading, axis, down)
        array = jnp.concatenate([before, array, after], axis=dim)
    return array


def add_partners(local):
    face = local.shape[0] // 4
    columns = local.shape[1]
    faces = local.reshape(4, face, columns)
    along_sub = extended(faces[0:2], (("sub", 0),), 1)
    along_grp = extended(faces[2:4], (("grp", 0),), 1)
    summed = jnp.stack(
        [
            faces[0] + along_sub[0],
            faces[1] + along_sub[3],
            faces[2] + along_grp[0],
            faces[3] + along_grp[3],
        ]
    )
    return summed.reshape(4 * face, columns)


def shards(
    schur_t, neumann_t, face_weights, coarse_basis, coarse_inverse, coarse_number, loads, iterate
):
    schur = schur_t[0, 0]
    neumann = neumann_t[0, 0]
    weights = face_weights[0, 0][:, None]
    basis = coarse_basis[0, 0]
    basis_wide = basis.astype(jnp.float32)
    basis_across = basis.T
    inverse_rows = coarse_inverse[0]
    numbers = coarse_number[0]
    per_sub = basis.shape[1]
    coarse_order = inverse_rows.shape[1]
    highest = lax.Precision.HIGHEST
    own = lax.dynamic_slice_in_dim(numbers, lax.axis_index("sub") * per_sub, per_sub)
    load_wide = loads[0, 0].astype(jnp.float32)
    current = iterate[0, 0]
    for step in range(ITERS):
        image = jnp.dot(schur, current, preferred_element_type=jnp.float32)
        resid = add_partners(load_wide - image)
        weighted = (weights * resid).astype(jnp.bfloat16)
        local_coarse = jnp.dot(basis_across, weighted, preferred_element_type=jnp.float32)
        scattered = jax.ops.segment_sum(local_coarse, own, num_segments=coarse_order)
        coarse_rhs = lax.psum(scattered, "sub")
        solved_rows = jnp.dot(inverse_rows, coarse_rhs, precision=highest)
        solved = lax.all_gather(solved_rows, "sub", axis=0, tiled=True)
        own_values = jnp.take(solved, own, axis=0)
        fine = jnp.dot(neumann, weighted, preferred_element_type=jnp.float32)
        correction = fine + jnp.dot(basis_wide, own_values, precision=highest)
        update = add_partners(weights * correction)
        current = (current.astype(jnp.float32) + update).astype(jnp.bfloat16)
    return current[None, None]


def solution(mesh):
    return jax.shard_map(
        shards,
        mesh=mesh,
        in_specs=(
            P("grp", "sub", None, None),
            P("grp", "sub", None, None),
            P("grp", "sub", None),
            P("grp", "sub", None, None),
            P("grp", "sub", None),
            P("grp", None),
            P("grp", "sub", None, None),
            P("grp", "sub", None, None),
        ),
        out_specs=P("grp", "sub", None, None),
        check_vma=False,
    )
```

profile of v0, /device:TPU:1, one launch (start us, length us, event | category | flops | bytes accessed | tf_op | source)
XLA Modules:
  0.0 2029.1 jit_solution(9209375182098139773)
XLA Ops:
  6.5 1.6 copy-done
  8.1 1.7 fusion.30
  10.6 5.6 collective-permute-start
  16.2 3.1 collective-permute-start.2
  19.3 4.3 collective-permute-start.3
  23.6 5.6 collective-permute-start.1
  32.3 1.0 fusion.67
  33.7 1.4 scatter_custom_fusion
  35.2 3.2 fusion.4
  38.4 537.9 %all-reduce.4.cloned.1.call-done = f32[768,128]{1,0:T(8,128)} async-done(((f32[768,128]{1,0:T(8,128)}), f32[768,128]{1,0:T(8,128)}) %all-reduce.4.cloned.1.call-update) | async-done | bytes 393232 | tf_op jit(solution)/shard_map/psum | solution.py:62
  576.3 1.3 convolution_bitcast_fusion.5
  577.6 79.9 %all-gather = f32[64,12,128]{2,1,0:T(8,128)S(1)} all-gather(f32[1,12,128]{2,1,0:T(8,128)S(1)} %convolution_bitcast_fusion.5), channel_id=1, replica_groups=mesh['grp'=8,'sub'=64] {'sub'}, dimensions={0}, use_global_device_ids=true | all-gather | bytes 399360 | tf_op jit(solution)/shard_map/all_gather | solution.py:64
  658.1 1.5 fusion.19
  659.6 0.8 slice_bitcast_fusion.18
  660.4 4.2 collective-permute-start.4
  664.6 2.1 collective-permute-start.6
  666.6 5.3 collective-permute-start.7
  672.0 1.9 collective-permute-start.5
  673.9 0.9 copy.20
  675.6 5.3 collective-permute-done.5
  680.9 1.2 fusion.71
  682.1 1.9 pad_maximum_fusion
  684.9 1.9 collective-permute-start.8
  686.8 1.9 collective-permute-start.10
  688.8 5.5 collective-permute-start.11
  694.3 3.0 collective-permute-start.9
  697.3 5.4 collective-permute-done.9
  703.1 1.4 scatter_custom_fusion.1
  704.6 3.2 fusion.2
  707.8 537.2 %all-reduce.6.cloned.1.call-done = f32[768,128]{1,0:T(8,128)} async-done(((f32[768,128]{1,0:T(8,128)}), f32[768,128]{1,0:T(8,128)}) %all-reduce.6.cloned.1.call-update) | async-done | bytes 393232 | tf_op jit(solution)/shard_map/psum | solution.py:62
  1245.0 1.3 convolution_bitcast_fusion.4
  1246.3 79.9 %all-gather.1 = f32[64,12,128]{2,1,0:T(8,128)S(1)} all-gather(f32[1,12,128]{2,1,0:T(8,128)S(1)} %convolution_bitcast_fusion.4), channel_id=1, replica_groups=mesh['grp'=8,'sub'=64] {'sub'}, dimensions={0}, use_global_device_ids=true | all-gather | bytes 399360 | tf_op jit(solution)/shard_map/all_gather | solution.py:64
  1326.1 0.8 reshape.405
  1326.9 1.6 gather_fusion.1
  1328.5 1.5 fusion.21
  1330.1 4.2 collective-permute-start.12
  1334.3 2.1 collective-permute-start.14
  1336.3 5.3 collective-permute-start.15
  1341.7 1.9 collective-permute-start.13
  1344.0 6.3 collective-permute-done.13
  1350.3 0.9 pad_maximum_fusion.1
  1352.1 1.9 collective-permute-start.16
  1354.1 1.9 collective-permute-start.18
  1356.0 5.5 collective-permute-start.19
  1361.5 3.0 collective-permute-start.17
  1364.5 5.4 collective-permute-done.17
  1370.3 1.4 scatter_custom_fusion.2
  1371.7 3.2 fusion
  1374.9 537.2 %all-reduce.8.cloned.1.call-done = f32[768,128]{1,0:T(8,128)} async-done(((f32[768,128]{1,0:T(8,128)}), f32[768,128]{1,0:T(8,128)}) %all-reduce.8.cloned.1.call-update) | async-done | bytes 393232 | tf_op jit(solution)/shard_map/psum | solution.py:62
  1912.1 1.3 convolution_bitcast_fusion.3
  1913.4 79.9 %all-gather.2 = f32[64,12,128]{2,1,0:T(8,128)S(1)} all-gather(f32[1,12,128]{2,1,0:T(8,128)S(1)} %convolution_bitcast_fusion.3), channel_id=1, replica_groups=mesh['grp'=8,'sub'=64] {'sub'}, dimensions={0}, use_global_device_ids=true | all-gather | bytes 399360 | tf_op jit(solution)/shard_map/all_gather | solution.py:64
  1994.1 1.6 gather_fusion.2
  1995.6 1.5 fusion.23
  1997.2 0.8 slice_bitcast_fusion.2
  1998.0 4.2 collective-permute-start.20
  2002.1 2.1 collective-permute-start.22
  2004.2 5.3 collective-permute-start.23
  2009.6 1.9 collective-permute-start.21
  2011.5 1.0 copy.19
  2012.5 2.0 copy.23
  2014.6 3.9 collective-permute-done.21
  2018.5 1.1 fusion.87
  2019.6 1.0 copy.26
  2020.6 2.0 add_convert_fusion
  (73 shorter events, 9.5 us)
Async XLA Ops:
  6.5 1.6 copy-start
  6.5 23.2 %copy-start.10 = (f32[1,1,1024]{2,1,0:T(1,128)S(1)}, f32[1,1,1024]{2,1,0:T(1,128)}, u32[]{:S(2)}) copy-start(f32[1,1,1024]{2,1,0:T(1,128)} %param.12) | copy-start | bytes 12292
  6.5 569.8 %all-reduce.4.cloned.1.call-start = ((), (), s32[]{:S(2)}) async-start(), calls=%async_computation | async-start | bytes 786432 | tf_op jit(solution)/shard_map/psum | solution.py:62
  9.9 23.6 %copy-start.5 = (bf16[1,1,1024,24]{2,3,1,0:T(8,128)(2,1)S(1)}, bf16[1,1,1024,24]{2,3,1,0:T(8,128)(2,1)}, u32[]{:S(2)}) copy-start(bf16[1,1,1024,24]{2,3,1,0:T(8,128)(2,1)} %param.13) | copy-start | bytes 147460
  10.6 20.5 %collective-permute-start = (f32[1,256,128]{2,1,0:T(8,128)}, f32[1,256,128]{2,1,0:T(8,128)S(1)}, u32[]{:S(2)}, u32[]{:S(2)}) collective-permute-start(f32[1,256,128]{2,1,0:T(8,128)} %get-tuple-element.56), channel_id=1, source_target_pairs={{0,1},{1,2},{2,3},{3,4},{4,5},{5,6},{6,7},{7,8},{8,9},{9,10},{10,1... | collective-permute-start | bytes 393224 | tf_op jit(solution)/shard_map/ppermute | solution.py:16
  16.2 14.9 collective-permute-start.2
  19.3 11.8 collective-permute-start.3
  23.6 8.7 collective-permute-start.1
  31.1 0.7 copy-start.7
  33.5 542.8 %copy-start.6 = (f32[1,12,768]{2,0,1:T(1,128)S(1)}, f32[1,12,768]{2,0,1:T(1,128)}, u32[]{:S(2)}) copy-start(f32[1,12,768]{2,0,1:T(1,128)} %param.14) | copy-start | bytes 110596
  35.1 1209.9 %all-reduce.6.cloned.1.call-start = ((), (), s32[]{:S(2)}) async-start(), calls=%async_computation.1 | async-start | bytes 786432 | tf_op jit(solution)/shard_map/psum | solution.py:62
  38.4 635.5 %copy-start.2 = (bf16[1,1,1024,128]{3,2,1,0:T(8,128)(2,1)S(1)}, bf16[1,1,1024,128]{3,2,1,0:T(8,128)(2,1)}, u32[]{:S(2)}) copy-start(bf16[1,1,1024,128]{3,2,1,0:T(8,128)(2,1)} %param.17) | copy-start | bytes 786436
  660.4 14.5 collective-permute-start.4
  664.6 10.3 collective-permute-start.6
  666.6 8.3 collective-permute-start.7
  672.0 8.9 collective-permute-start.5
  674.9 9.3 copy-start.1
  674.9 0.7 copy-start.8
  674.9 0.7 copy-start.9
  684.9 12.3 collective-permute-start.8
  686.8 10.4 collective-permute-start.10
  688.8 8.5 collective-permute-start.11
  694.3 8.4 collective-permute-start.9
  704.5 1207.6 %all-reduce.8.cloned.1.call-start = ((), (), s32[]{:S(2)}) async-start(), calls=%async_computation.2 | async-start | bytes 786432 | tf_op jit(solution)/shard_map/psum | solution.py:62
  1330.1 13.5 collective-permute-start.12
  1334.3 9.3 collective-permute-start.14
  1336.3 7.6 collective-permute-start.15
  1341.7 8.6 collective-permute-start.13
  1352.1 12.3 collective-permute-start.16
  1354.1 10.4 collective-permute-start.18
  1356.0 8.5 collective-permute-start.19
  1361.5 8.4 collective-permute-start.17
  1374.9 636.5 %copy-start.3 = (f32[4,256,128]{1,2,0:T(8,128)S(1)}, f32[4,256,128]{1,2,0:T(8,128)}, u32[]{:S(2)}) copy-start(f32[4,256,128]{1,2,0:T(8,128)} %get-tuple-element.8) | copy-start | bytes 1572868
  1998.0 16.6 collective-permute-start.20
  2002.1 12.4 collective-permute-start.22
  2004.2 10.3 collective-permute-start.23
  2009.6 8.9 collective-permute-start.21
  2014.5 6.1 copy-start.4
Sparse Core Ops, SparseCore 0:
  35.2 541.0 all-reduce.3
  704.7 540.2 all-reduce.5
  1371.8 540.2 all-reduce.7
where the time goes:
time: 2030 us
  waiting for transfers between devices  1640 us (81%)
  blocking collectives  240 us (12%)
  starting transfers between devices  83.7 us (4%)
  matrix products  21.8 us (1%)
    psum x3, waiting for transfers between devices, shards(): coarse_rhs = lax.psum(scattered, 'sub')  1610 us
    all_gather x3, blocking collectives, shards(): solved = lax.all_gather(solved_rows, 'sub', axis=0, tiled=True)  240 us
    ppermute x12, starting transfers between devices, extended(): after = lax.ppermute(leading, axis, down)  48.5 us
  transfers between devices with their start and end apart: 27, of which 10 were waited for; matrix products, arithmetic and copies ran while one was open for 1% of the time, Pallas kernels for 0%

commit v1 on v0

v1 whole, which is shorter than its diff:
```python
import jax
import jax.numpy as jnp
from jax import lax
from jax.experimental import pallas as pl
from jax.experimental.pallas import tpu as pltpu
from jax.sharding import PartitionSpec as P

ITERS = 3
FACE = 256
MESH = pl.DeviceIdType.MESH
FAR_FIRST = (4, 3, 5, 2, 6, 1, 7)
F32, BF16 = jnp.float32, jnp.bfloat16


def dot(a, b):
    return jnp.dot(a, b, preferred_element_type=F32)


def halves(x):
    high = x.astype(BF16)
    return high, (x - high.astype(F32)).astype(BF16)


def kernel(
    s_hbm, n_hbm, w_hbm, bt_hbm, inv_hbm, num_hbm, l_hbm, x_hbm, o_ref,
    s_ref, n_ref, w_ref, bt_ref, inv_ref, num_ref, l_ref, wb, bb, wt, u_keep, inv16, planes, turns, cols_ref, rows_ref,
    ex_src, ex_dst, up_src, up_dst, c_all, part, part_in, own_src, own_dst,
    ga_src, ga_dst, slab1, slab2, all1, all2, a_hi, a_lo, nb_src, nb_dst,
    load_sem, ex_s, ex_r, up_s, up_r, c1_s, c1_r, c2_s, c2_r, ow_s, ow_r, ga_s, ga_r, gb_s, gb_r, nb_s, nb_r,
):
    g, s = lax.axis_index("grp"), lax.axis_index("sub")
    z, yc = s // 8, s % 8
    near = [(g, (s + 63) % 64), (g, (s + 1) % 64), ((g + 7) % 8, s), ((g + 1) % 8, s)]
    mate = [1, 0, 3, 2]

    def z_peer(k):
        return (g, ((z + k) % 8) * 8 + yc)

    def yc_peer(k):
        return (g, z * 8 + (yc + k) % 8)

    def rc(src, dst, ssem, rsem, dev):
        return pltpu.make_async_remote_copy(
            src_ref=src, dst_ref=dst, send_sem=ssem, recv_sem=rsem, device_id=dev, device_id_type=MESH
        )

    def face(f):
        return pl.ds(f * FACE, FACE)

    def ex_copy(it, f):
        m = mate[f]
        return rc(ex_src.at[it, face(f)], ex_dst.at[it, face(m)], ex_s.at[it, f], ex_r.at[it, m], near[f])

    def up_copy(it, f):
        m = mate[f]
        return rc(up_src.at[it, face(f)], up_dst.at[it, face(m)], up_s.at[it, f], up_r.at[it, m], near[f])

    def ow_copy(it, f):
        m = mate[f]
        return rc(own_src.at[it], own_dst.at[it, m], ow_s.at[it, f], ow_r.at[it, m], near[f])

    def nb_copy(f):
        m = mate[f]
        return rc(nb_src.at[f], nb_dst.at[m], nb_s.at[f], nb_r.at[m], near[f])

    def c1_copy(it, k):
        mine = pl.ds(pl.multiple_of(z * 24, 8), 24)
        return rc(c_all.at[it, mine], c_all.at[it, mine], c1_s.at[it, k], c1_r.at[it, k], z_peer(k))

    def c2_copy(it, k):
        there = pl.ds(pl.multiple_of(((yc + k) % 8) * 24, 8), 24)
        return rc(part.at[it, there], part_in.at[it, k], c2_s.at[it, k], c2_r.at[it, k], yc_peer(k))

    def ga_copy(k):
        return rc(ga_src.at[(yc + k) % 8], ga_dst.at[yc], ga_s.at[k], ga_r.at[k], yc_peer(k))

    def gb_copy(k):
        here = pl.ds(pl.multiple_of(z * 96, 8), 96)
        return rc(slab1, all1.at[here], gb_s.at[0, k], gb_r.at[0, k], z_peer(k))

    def gc_copy(k):
        here = pl.ds(pl.multiple_of(z * 48, 8), 48)
        return rc(slab2, all2.at[here], gb_s.at[1, k], gb_r.at[1, k], z_peer(k))

    load_s, load_n, load_w, load_bt, load_inv, load_num, load_l, load_x = [
        pltpu.make_async_copy(a, b, load_sem.at[i])
        for i, (a, b) in enumerate(
            [(s_hbm, s_ref), (n_hbm, n_ref), (w_hbm, w_ref), (bt_hbm, bt_ref), (inv_hbm, inv_ref),
             (num_hbm, num_ref), (l_hbm, l_ref), (x_hbm, o_ref)]
        )
    ]
    for load in (load_num, load_inv, load_bt, load_w, load_x, load_s, load_l, load_n):
        load.start()
    c_all[...] = jnp.zeros_like(c_all)

    barrier = pltpu.get_barrier_semaphore()
    for dev in near + [z_peer(k) for k in range(1, 8)] + [yc_peer(k) for k in range(1, 8)]:
        pl.semaphore_signal(barrier, inc=1, device_id=dev, device_id_type=MESH)

    load_num.wait()
    for q in range(8):
        at = (192 * q) // 128 * 128
        row = num_ref[:, at : at + 256]
        planes[q : q + 1, :] = row if q % 2 == 0 else pltpu.roll(row, 192, axis=1)
    for q in range(8):
        turned = planes[...] if q == 0 else pltpu.roll(planes[...], 256 - 24 * q, axis=1)
        for p in range(8):
            turns[p, q : q + 1, :] = turned[p : p + 1, :]
    lane = lax.broadcasted_iota(jnp.int32, (8, 256), 1)
    cols = jnp.where(lane < 24, turns[0], -1)
    for p in range(1, 8):
        here = (lane >= 24 * p) & (lane < 24 * p + 24)
        cols = jnp.where(here, pltpu.roll(turns[p], 24 * p, axis=1), cols)
    cols_ref[...] = cols
    n = planes[pl.ds(z, 1), :]
    zn = (n * 683) >> 16
    dn = (n * 5462) >> 16
    i, dn = n - 12 * dn, dn - 8 * zn
    r = jnp.where(i < 8, dn * 8 + i, 56 + dn * 4 + i)
    rows_ref[0:1, :] = zn * 96 + r
    rows_ref[1:2, :] = jnp.where(r < 48, zn * 48 + r, -1)
    rows_ref[2:3, :] = jnp.where(r >= 48, zn * 48 + r - 48, -1)

    load_inv.wait()
    inv16[...] = jnp.zeros_like(inv16)
    for q in range(8):
        inv16[q : q + 1, :] = inv_ref[q]
    for q in range(8, 12):
        inv16[pl.ds(q + 4 * (yc % 2), 1), :] = inv_ref[q]
    inv_hi, inv_lo = halves(inv16[...])
    pieces = jnp.concatenate([inv_hi, inv_lo], axis=0)
    order = lax.broadcasted_iota(jnp.int32, (768, 256), 0)

    def pick(q, carry):
        hot = jnp.where(order == cols_ref[pl.ds(q, 1), :], 1.0, 0.0).astype(BF16)
        both = dot(pieces, hot)
        ga_src[q] = both[:16] + both[16:]
        return carry

    lax.fori_loop(0, 8, pick, 0)
    load_bt.wait()
    basis = bt_ref[...].astype(F32)
    for f in range(4):
        nb_src[f] = basis[:, f * FACE : (f + 1) * FACE]

    pl.semaphore_wait(barrier, 18)
    for k in FAR_FIRST:
        ga_copy(k).start()
    ga_dst[yc] = ga_src[yc]
    for f in range(4):
        nb_copy(f).start()

    load_w.wait()
    for q in range(8):
        wide = jnp.broadcast_to(w_ref[q : q + 1, :], (128, 128))
        wb[q * 128 : (q + 1) * 128, :] = wide.T

    load_x.wait()
    load_s.wait()
    load_l.wait()

    def send_part(it, current):
        for f in (1, 0, 3, 2):
            image = dot(s_ref[face(f), :], current)
            ex_src[it, face(f), :] = l_ref[face(f), :].astype(F32) - image
            ex_copy(it, f).start()

    def make_slabs():
        for k in range(1, 8):
            ga_copy(k).wait_recv()
        low = [ga_dst[q, 0:8, :] for q in range(8)]
        high = [ga_dst[2 * q, 8:16, :] + ga_dst[2 * q + 1, 8:16, :] for q in range(4)]
        slab = jnp.concatenate(low + high, axis=0)
        slab1[...] = slab[:, 0:128]
        slab2[...] = slab[0:48, 128:256] + pltpu.roll(slab[48:96, 128:256], 64, axis=1)
        for k in FAR_FIRST:
            gb_copy(k).start()
            gc_copy(k).start()
        all1[pl.ds(pl.multiple_of(z * 96, 8), 96), :] = slab1[...]
        all2[pl.ds(pl.multiple_of(z * 48, 8), 48), :] = slab2[...]

    def make_basis():
        for f in range(4):
            nb_copy(f).wait_recv()
        for f in range(4):
            own, other = nb_src[f], nb_dst[f]
            rows = jnp.concatenate([own, own, other, other, jnp.zeros((32, FACE), F32)], axis=0)
            for h in range(2):
                at = f * FACE + h * 128
                bb[at : at + 128, :] = rows[:, h * 128 : (h + 1) * 128].T.astype(BF16)

    def make_a():
        for k in range(1, 8):
            gb_copy(k).wait_recv()
            gc_copy(k).wait_recv()

        def column(at):
            return jnp.broadcast_to(rows_ref[at : at + 1, :], (128, 256)).T[0:192, :]

        def hot(at, width):
            wanted = column(at)
            lane = lax.broadcasted_iota(jnp.int32, (192, 128), 1)
            return jnp.concatenate(
                [jnp.where(wanted == lane + 128 * i, 1.0, 0.0).astype(BF16) for i in range(width // 128)], axis=1
            )

        first = dot(hot(0, 768), jnp.concatenate(halves(all1[...]), axis=1))
        two = jnp.concatenate(halves(all2[...]), axis=1)
        left, right = dot(hot(1, 384), two), dot(hot(2, 384), two)
        lane = lax.broadcasted_iota(jnp.int32, (192, 128), 1)
        for out, at in ((a_hi, 0), (a_lo, 128)):
            tail = left[:, at : at + 128] + 0.0
            other = pltpu.roll(right[:, at : at + 128], 64, axis=1)
            tail = jnp.where(lane < 64, tail, 0.0) + jnp.where(lane < 64, other, 0.0)
            out[...] = jnp.concatenate([first[:, at : at + 128], tail], axis=1).astype(BF16)

    def step(it, carry):
        @pl.when(it == 0)
        def _():
            make_slabs()

        mine = pl.ds(pl.multiple_of(z * 24, 8), 24)
        local = jnp.zeros((24, 128), F32)
        for f in (2, 3, 0, 1):
            ex_copy(it, mate[f]).wait_recv()
            resid = ex_src[it, face(f), :] + ex_dst[it, face(f), :]
            weighted = (wb[face(f), :] * resid).astype(BF16)
            wt[face(f), :] = weighted
            local = local + dot(bt_ref[:, f * FACE : (f + 1) * FACE], weighted)
        c_all[it, mine, :] = local
        for k in FAR_FIRST:
            c1_copy(it, k).start()

        @pl.when(it == 0)
        def _():
            load_n.wait()

        for f in (1, 0, 3, 2):
            up_src[it, face(f), :] = wb[face(f), :] * dot(n_ref[face(f), :], wt[...])
            up_copy(it, f).start()

        @pl.when(it == 0)
        def _():
            make_basis()
            make_a()

        for k in range(1, 8):
            c1_copy(it, k).wait_recv()
        high, low = halves(c_all[it])
        part[it] = dot(a_hi[...], high) + dot(a_hi[...], low) + dot(a_lo[...], high)
        for k in FAR_FIRST:
            c2_copy(it, k).start()
        total = part[it, pl.ds(pl.multiple_of(yc * 24, 8), 24), :]
        for k in range(1, 8):
            c2_copy(it, k).wait_recv()
            total = total + part_in[it, k]
        own_src[it] = total
        for f in (1, 0, 3, 2):
            ow_copy(it, f).start()
        for f in range(4):
            up_copy(it, mate[f]).wait_recv()
            u_keep[face(f), :] = x_now[face(f), :].astype(F32) + (up_src[it, face(f), :] + up_dst[it, face(f), :])
        own_hi = total.astype(BF16).astype(F32)
        zeros24, zeros80 = jnp.zeros((48, 128), F32), jnp.zeros((80, 128), F32)
        for f in (2, 3, 0, 1):
            ow_copy(it, mate[f]).wait_recv()
            other = own_dst[it, f]
            other_hi = other.astype(BF16).astype(F32)
            mine_in = jnp.concatenate([own_hi, total - own_hi, zeros80], axis=0).astype(BF16)
            other_in = jnp.concatenate([zeros24, other_hi, other - other_hi, zeros80[:32]], axis=0).astype(BF16)
            w = wb[face(f), :]
            coarse = w * dot(bb[face(f), :], mine_in) + (1.0 - w) * dot(bb[face(f), :], other_in)
            x_now[face(f), :] = (u_keep[face(f), :] + coarse).astype(BF16)

        @pl.when(it + 1 < ITERS)
        def _():
            send_part(it + 1, x_now[...])

        return carry

    x_now = o_ref
    send_part(0, x_now[...])
    lax.fori_loop(0, ITERS, step, 0)

    def drain(it, carry):
        for f in range(4):
            ex_copy(it, f).wait_send()
            up_copy(it, f).wait_send()
            ow_copy(it, f).wait_send()
        for k in range(1, 8):
            c1_copy(it, k).wait_send()
            c2_copy(it, k).wait_send()
        return carry

    lax.fori_loop(0, ITERS, drain, 0)
    for f in range(4):
        nb_copy(f).wait_send()
    for k in range(1, 8):
        ga_copy(k).wait_send()
        gb_copy(k).wait_send()
        gc_copy(k).wait_send()


def shards(schur_t, neumann_t, face_weights, coarse_basis, coarse_inverse, coarse_number, loads, iterate):
    weights = face_weights.reshape(8, 128)
    basis_t = coarse_basis[0, 0].T
    vmem = pl.BlockSpec(memory_space=pltpu.VMEM)
    hbm = pl.BlockSpec(memory_space=pl.ANY)
    dma = pltpu.SemaphoreType.DMA
    out = pl.pallas_call(
        kernel,
        name="bddc_steps",
        out_shape=jax.ShapeDtypeStruct((1024, 128), BF16),
        in_specs=[hbm] * 8,
        out_specs=vmem,
        scratch_shapes=[
            pltpu.VMEM((1024, 1024), BF16),
            pltpu.VMEM((1024, 1024), BF16),
            pltpu.VMEM((8, 128), F32),
            pltpu.VMEM((24, 1024), BF16),
            pltpu.VMEM((12, 1, 768), F32),
            pltpu.VMEM((1, 1536), jnp.int32),
            pltpu.VMEM((1024, 128), BF16),
            pltpu.VMEM((1024, 128), F32),
            pltpu.VMEM((1024, 128), BF16),
            pltpu.VMEM((1024, 128), BF16),
            pltpu.VMEM((1024, 128), F32),
            pltpu.VMEM((16, 768), F32),
            pltpu.VMEM((8, 256), jnp.int32),
            pltpu.VMEM((8, 8, 256), jnp.int32),
            pltpu.VMEM((8, 256), jnp.int32),
            pltpu.VMEM((8, 256), jnp.int32),
            pltpu.VMEM((ITERS, 1024, 128), F32),
            pltpu.VMEM((ITERS, 1024, 128), F32),
            pltpu.VMEM((ITERS, 1024, 128), F32),
            pltpu.VMEM((ITERS, 1024, 128), F32),
            pltpu.VMEM((ITERS, 256, 128), F32),
            pltpu.VMEM((ITERS, 192, 128), F32),
            pltpu.VMEM((ITERS, 8, 24, 128), F32),
            pltpu.VMEM((ITERS, 24, 128), F32),
            pltpu.VMEM((ITERS, 4, 24, 128), F32),
            pltpu.VMEM((8, 16, 256), F32),
            pltpu.VMEM((8, 16, 256), F32),
            pltpu.VMEM((96, 128), F32),
            pltpu.VMEM((48, 128), F32),
            pltpu.VMEM((768, 128), F32),
            pltpu.VMEM((384, 128), F32),
            pltpu.VMEM((192, 256), BF16),
            pltpu.VMEM((192, 256), BF16),
            pltpu.VMEM((4, 24, 256), F32),
            pltpu.VMEM((4, 24, 256), F32),
            dma((8,)),
            dma((ITERS, 4)), dma((ITERS, 4)),
            dma((ITERS, 4)), dma((ITERS, 4)),
            dma((ITERS, 8)), dma((ITERS, 8)),
            dma((ITERS, 8)), dma((ITERS, 8)),
            dma((ITERS, 4)), dma((ITERS, 4)),
            dma((8,)), dma((8,)),
            dma((2, 8)), dma((2, 8)),
            dma((4,)), dma((4,)),
        ],
        compiler_params=pltpu.CompilerParams(
            collective_id=0, has_side_effects=True, vmem_limit_bytes=67000000
        ),
    )(schur_t[0, 0], neumann_t[0, 0], weights, basis_t, coarse_inverse.reshape(12, 1, 768), coarse_number, loads[0, 0], iterate[0, 0])
    return out[None, None]


def solution(mesh):
    return jax.shard_map(
        shards,
        mesh=mesh,
        in_specs=(
            P("grp", "sub", None, None),
            P("grp", "sub", None, None),
            P("grp", "sub", None),
            P("grp", "sub", None, None),
            P("grp", "sub", None),
            P("grp", None),
            P("grp", "sub", None, None),
            P("grp", "sub", None, None),
        ),
        out_specs=P("grp", "sub", None, None),
        check_vma=False,
    )
```

time: 2030 us -> 104 us (0.05)
  waiting for transfers between devices: 1640 us -> 0 us
  blocking collectives: 240 us -> 0 us
  Pallas kernels: 0 us -> 102 us
  starting transfers between devices: 83.7 us -> 0 us
  matrix products: 21.8 us -> 0 us
    psum x3 -> x0, waiting for transfers between devices: 1610 us -> none  [shards(): coarse_rhs = lax.psum(scattered, 'sub')]
    all_gather x3 -> x0, blocking collectives: 240 us -> none  [shards(): solved = lax.all_gather(solved_rows, 'sub', axis=0, tiled=True)]
    pallas_call x0 -> x1, Pallas kernels: none -> 102 us  [shards(): pl.pallas_call(kernel, name='bddc_steps', out_shape=jax.ShapeDtypeStruct(...]
    ppermute x24 -> x0, starting transfers between devices: 83.6 us -> none  [the longest x12 48.5 us: extended(): after = lax.ppermute(leading, axis, down)]
    ppermute x24 -> x0, waiting for transfers between devices: 27.2 us -> none  [the longest x12 27.2 us: extended(): after = lax.ppermute(leading, axis, down)]
    dot_general x15 -> x0, matrix products: 21.8 us -> none  [the longest x3 9.66 us: shards(): fine = jnp.dot(neumann, weighted, preferred_element_type=jnp.float32)]
  transfers between devices with their start and end apart: 27 -> 0, of which waited for: 10 -> 0; matrix products, arithmetic and copies ran while one was open for 1% -> 0% of each run, Pallas kernels for 0% -> 0%
where the time goes in v1:
time: 104 us; the launch traced here: 103 us
  Pallas kernels  102 us (98%)
  local copies, waits for them, and re-layouts  1.67 us (2%)
    pallas_call x1, Pallas kernels, shards(): pl.pallas_call(kernel, name='bddc_steps', out_shape=jax.ShapeDtypeStruct(...  102 us

profile of v1, /device:TPU:1, one launch (start us, length us, event | category | flops | bytes accessed | tf_op | source)
XLA Modules:
  0.0 103.4 jit_solution(6021843570413421669)
XLA Ops:
  0.0 101.7 %bddc_steps.1 = bf16[1024,128]{1,0:T(8,128)(2,1)} custom-call(bf16[1024,1024]{1,0:T(8,128)(2,1)} %bitcast.10, bf16[1024,1024]{1,0:T(8,128)(2,1)} %bitcast.11, f32[8,128]{1,0:T(8,128)} %bitcast.17, bf16[24,1024]{1,0:T(8,128)(2,1)} %bitcast.15, f32[12,1,768]{2,1,0:T(1,128)} %bitcast.16, s32[1,1536]{1,0:T(1,128)} %num_hbm.1, bf16[1024,128]{1,0:T(8,128)(2,1)} %bitcast.13, ...), custom_call_target="tpu_custom_call" | custom-call | tf_op jit(solution)/shard_map/bddc_steps/pallas_call | solution.py:310
  101.7 1.7 %copy.10 = bf16[1,1,1024,128]{3,2,1,0:T(8,128)(2,1)} copy(bf16[1,1,1024,128]{3,2,1,0:T(8,128)(2,1)} %bitcast.12) | data formatting | bytes 524288

commit v2 on v1

--- a/solution.py
+++ b/solution.py
@@ -9,6 +9,18 @@
 FACE = 256
 MESH = pl.DeviceIdType.MESH
 FAR_FIRST = (4, 3, 5, 2, 6, 1, 7)
+AROUND = (
+    (0, 0), (0, -1), (0, 1), (-1, 0), (1, 0),
+    (0, -2), (0, 2), (-2, 0), (2, 0), (-1, -1), (-1, 1), (1, -1), (1, 1),
+)
+
+
+def place(*steps):
+    return AROUND.index((sum(a for a, _ in steps), sum(b for _, b in steps)))
+
+
+FIVE = [[place(AROUND[i], AROUND[j]) for j in range(5)] for i in range(5)]
+BACK = [AROUND.index((-a, -b)) for a, b in AROUND]
 F32, BF16 = jnp.float32, jnp.bfloat16
 
 
@@ -23,15 +35,16 @@
 
 def kernel(
     s_hbm, n_hbm, w_hbm, bt_hbm, inv_hbm, num_hbm, l_hbm, x_hbm, o_ref,
-    s_ref, n_ref, w_ref, bt_ref, inv_ref, num_ref, l_ref, wb, bb, wt, u_keep, inv16, planes, turns, cols_ref, rows_ref,
-    ex_src, ex_dst, up_src, up_dst, c_all, part, part_in, own_src, own_dst,
+    s_ref, n_ref, w_ref, bt_ref, inv_ref, num_ref, l_ref, wb, b5, wt, x_fine, corr, t_src, t_dst, t_hi, t_lo, inv16, planes, turns, cols_ref, rows_ref,
+    ex_src, ex_dst, up_src, up_dst, c_all, part, part_in, own,
     ga_src, ga_dst, slab1, slab2, all1, all2, a_hi, a_lo, nb_src, nb_dst,
-    load_sem, ex_s, ex_r, up_s, up_r, c1_s, c1_r, c2_s, c2_r, ow_s, ow_r, ga_s, ga_r, gb_s, gb_r, nb_s, nb_r,
+    load_sem, ex_s, ex_r, up_s, up_r, c1_s, c1_r, c2_s, c2_r, ow_s, ow_r, ga_s, ga_r, gb_s, gb_r, nb_s, nb_r, t_s, t_r,
 ):
     g, s = lax.axis_index("grp"), lax.axis_index("sub")
     z, yc = s // 8, s % 8
     near = [(g, (s + 63) % 64), (g, (s + 1) % 64), ((g + 7) % 8, s), ((g + 1) % 8, s)]
     mate = [1, 0, 3, 2]
+    around = [((g + (8 + dg)) % 8, (s + (64 + ds)) % 64) for dg, ds in AROUND[1:]]
 
     def z_peer(k):
         return (g, ((z + k) % 8) * 8 + yc)
@@ -55,9 +68,14 @@
         m = mate[f]
         return rc(up_src.at[it, face(f)], up_dst.at[it, face(m)], up_s.at[it, f], up_r.at[it, m], near[f])
 
-    def ow_copy(it, f):
+    def ow_copy(it, i):
+        dg, ds = AROUND[i]
+        there = ((g + (8 + dg)) % 8, (s + (64 + ds)) % 64)
+        return rc(own.at[it, 0], own.at[it, BACK[i]], ow_s.at[it, i], ow_r.at[it, BACK[i]], there)
+
+    def t_copy(f):
         m = mate[f]
-        return rc(own_src.at[it], own_dst.at[it, m], ow_s.at[it, f], ow_r.at[it, m], near[f])
+        return rc(t_src.at[face(f)], t_dst.at[face(m)], t_s.at[f], t_r.at[m], near[f])
 
     def nb_copy(f):
         m = mate[f]
@@ -92,9 +110,10 @@
     for load in (load_num, load_inv, load_bt, load_w, load_x, load_s, load_l, load_n):
         load.start()
     c_all[...] = jnp.zeros_like(c_all)
+    corr[...] = jnp.zeros_like(corr)
 
     barrier = pltpu.get_barrier_semaphore()
-    for dev in near + [z_peer(k) for k in range(1, 8)] + [yc_peer(k) for k in range(1, 8)]:
+    for dev in around + [z_peer(k) for k in range(1, 8)] + [yc_peer(k) for k in range(1, 8)]:
         pl.semaphore_signal(barrier, inc=1, device_id=dev, device_id_type=MESH)
 
     load_num.wait()
@@ -143,7 +162,7 @@
     for f in range(4):
         nb_src[f] = basis[:, f * FACE : (f + 1) * FACE]
 
-    pl.semaphore_wait(barrier, 18)
+    pl.semaphore_wait(barrier, 26)
     for k in FAR_FIRST:
         ga_copy(k).start()
     ga_dst[yc] = ga_src[yc]
@@ -182,12 +201,38 @@
     def make_basis():
         for f in range(4):
             nb_copy(f).wait_recv()
-        for f in range(4):
-            own, other = nb_src[f], nb_dst[f]
-            rows = jnp.concatenate([own, own, other, other, jnp.zeros((32, FACE), F32)], axis=0)
+        lane = lax.broadcasted_iota(jnp.int32, (128, 128), 1)
+        none = jnp.zeros((24, FACE), F32)
+        for f in range(4):
+            rows = [nb_src[f]] + [nb_dst[f] if j == f else none for j in range(4)] + [none[:8]]
+            rows = jnp.concatenate(rows, axis=0)
             for h in range(2):
                 at = f * FACE + h * 128
-                bb[at : at + 128, :] = rows[:, h * 128 : (h + 1) * 128].T.astype(BF16)
+                w = wb[at : at + 128, :]
+                scaled = jnp.where(lane < 24, w, 1.0 - w) * rows[:, h * 128 : (h + 1) * 128].T
+                b5[at : at + 128, :] = jnp.concatenate(halves(scaled), axis=1)
+        for f in (1, 0, 3, 2):
+            both = dot(s_ref[face(f), :], b5[...])
+            t_src[face(f), :] = both[:, :128] + both[:, 128:]
+            t_copy(f).start()
+
+    def make_t():
+        for f in range(4):
+            t_copy(mate[f]).wait_recv()
+            (mine_hi, mine_lo), (other_hi, other_lo) = halves(t_src[face(f), :]), halves(t_dst[face(f), :])
+            t_hi[face(f), :] = jnp.concatenate([mine_hi, other_hi], axis=1)
+            t_lo[face(f), :] = jnp.concatenate([mine_lo, other_lo], axis=1)
+
+    def five(it, i):
+        return [own[it, j] for j in FIVE[i]] + [jnp.zeros((8, 128), F32)]
+
+    def finish(it):
+        high, low = halves(jnp.concatenate(five(it, 0), axis=0))
+        pair = jnp.concatenate([high, low], axis=1)
+        for f in range(4):
+            both = dot(b5[face(f), 0:128], pair)
+            coarse = both[:, :128] + both[:, 128:] + dot(b5[face(f), 128:256], high)
+            x_now[face(f), :] = (x_fine[face(f), :] + coarse).astype(BF16)
 
     def make_a():
         for k in range(1, 8):
@@ -223,7 +268,7 @@
         local = jnp.zeros((24, 128), F32)
         for f in (2, 3, 0, 1):
             ex_copy(it, mate[f]).wait_recv()
-            resid = ex_src[it, face(f), :] + ex_dst[it, face(f), :]
+            resid = ex_src[it, face(f), :] + ex_dst[it, face(f), :] - corr[face(f), :]
             weighted = (wb[face(f), :] * resid).astype(BF16)
             wt[face(f), :] = weighted
             local = local + dot(bt_ref[:, f * FACE : (f + 1) * FACE], weighted)
@@ -244,57 +289,78 @@
             make_basis()
             make_a()
 
+        @pl.when(it > 0)
+        def _():
+            finish(it - 1)
+
         for k in range(1, 8):
             c1_copy(it, k).wait_recv()
         high, low = halves(c_all[it])
         part[it] = dot(a_hi[...], high) + dot(a_hi[...], low) + dot(a_lo[...], high)
         for k in FAR_FIRST:
             c2_copy(it, k).start()
+        for f in range(4):
+            up_copy(it, mate[f]).wait_recv()
+            x_fine[face(f), :] = x_now[face(f), :].astype(F32) + (up_src[it, face(f), :] + up_dst[it, face(f), :])
+
+        @pl.when(it + 1 < ITERS)
+        def _():
+            send_part(it + 1, x_fine[...].astype(BF16))
+
         total = part[it, pl.ds(pl.multiple_of(yc * 24, 8), 24), :]
         for k in range(1, 8):
             c2_copy(it, k).wait_recv()
             total = total + part_in[it, k]
-        own_src[it] = total
-        for f in (1, 0, 3, 2):
-            ow_copy(it, f).start()
-        for f in range(4):
-            up_copy(it, mate[f]).wait_recv()
-            u_keep[face(f), :] = x_now[face(f), :].astype(F32) + (up_src[it, face(f), :] + up_dst[it, face(f), :])
-        own_hi = total.astype(BF16).astype(F32)
-        zeros24, zeros80 = jnp.zeros((48, 128), F32), jnp.zeros((80, 128), F32)
-        for f in (2, 3, 0, 1):
-            ow_copy(it, mate[f]).wait_recv()
-            other = own_dst[it, f]
-            other_hi = other.astype(BF16).astype(F32)
-            mine_in = jnp.concatenate([own_hi, total - own_hi, zeros80], axis=0).astype(BF16)
-            other_in = jnp.concatenate([zeros24, other_hi, other - other_hi, zeros80[:32]], axis=0).astype(BF16)
-            w = wb[face(f), :]
-            coarse = w * dot(bb[face(f), :], mine_in) + (1.0 - w) * dot(bb[face(f), :], other_in)
-            x_now[face(f), :] = (u_keep[face(f), :] + coarse).astype(BF16)
+        own[it, 0] = total
+        for i in (2, 1, 4, 3):
+            ow_copy(it, i).start()
 
         @pl.when(it + 1 < ITERS)
         def _():
-            send_part(it + 1, x_now[...])
+            for i in (9, 10, 11, 12, 5, 6, 7, 8):
+                ow_copy(it, i).start()
+
+            @pl.when(it == 0)
+            def _():
+                make_t()
+
+            for i in range(1, 13):
+                ow_copy(it, i).wait_recv()
+            here = five(it, 0)
+            for f in range(4):
+                high, low = halves(jnp.concatenate(here + five(it, 1 + f), axis=0))
+                both = dot(t_hi[face(f), :], jnp.concatenate([high, low], axis=1))
+                corr[face(f), :] = both[:, :128] + both[:, 128:] + dot(t_lo[face(f), :], high)
 
         return carry
 
     x_now = o_ref
     send_part(0, x_now[...])
     lax.fori_loop(0, ITERS, step, 0)
+    for i in range(1, 5):
+        ow_copy(ITERS - 1, i).wait_recv()
+    finish(ITERS - 1)
 
     def drain(it, carry):
         for f in range(4):
             ex_copy(it, f).wait_send()
             up_copy(it, f).wait_send()
-            ow_copy(it, f).wait_send()
+            ow_copy(it, f + 1).wait_send()
         for k in range(1, 8):
             c1_copy(it, k).wait_send()
             c2_copy(it, k).wait_send()
+
+        @pl.when(it + 1 < ITERS)
+        def _():
+            for i in range(5, 13):
+                ow_copy(it, i).wait_send()
+
         return carry
 
     lax.fori_loop(0, ITERS, drain, 0)
     for f in range(4):
         nb_copy(f).wait_send()
+        t_copy(f).wait_send()
     for k in range(1, 8):
         ga_copy(k).wait_send()
         gb_copy(k).wait_send()
@@ -322,9 +388,14 @@
             pltpu.VMEM((1, 1536), jnp.int32),
             pltpu.VMEM((1024, 128), BF16),
             pltpu.VMEM((1024, 128), F32),
-            pltpu.VMEM((1024, 128), BF16),
+            pltpu.VMEM((1024, 256), BF16),
             pltpu.VMEM((1024, 128), BF16),
             pltpu.VMEM((1024, 128), F32),
+            pltpu.VMEM((1024, 128), F32),
+            pltpu.VMEM((1024, 128), F32),
+            pltpu.VMEM((1024, 128), F32),
+            pltpu.VMEM((1024, 256), BF16),
+            pltpu.VMEM((1024, 256), BF16),
             pltpu.VMEM((16, 768), F32),
             pltpu.VMEM((8, 256), jnp.int32),
             pltpu.VMEM((8, 8, 256), jnp.int32),
@@ -337,8 +408,7 @@
             pltpu.VMEM((ITERS, 256, 128), F32),
             pltpu.VMEM((ITERS, 192, 128), F32),
             pltpu.VMEM((ITERS, 8, 24, 128), F32),
-            pltpu.VMEM((ITERS, 24, 128), F32),
-            pltpu.VMEM((ITERS, 4, 24, 128), F32),
+            pltpu.VMEM((ITERS, 13, 24, 128), F32),
             pltpu.VMEM((8, 16, 256), F32),
             pltpu.VMEM((8, 16, 256), F32),
             pltpu.VMEM((96, 128), F32),
@@ -354,9 +424,10 @@
             dma((ITERS, 4)), dma((ITERS, 4)),
             dma((ITERS, 8)), dma((ITERS, 8)),
             dma((ITERS, 8)), dma((ITERS, 8)),
-            dma((ITERS, 4)), dma((ITERS, 4)),
+            dma((ITERS, 13)), dma((ITERS, 13)),
             dma((8,)), dma((8,)),
             dma((2, 8)), dma((2, 8)),
+            dma((4,)), dma((4,)),
             dma((4,)), dma((4,)),
         ],
         compiler_params=pltpu.CompilerParams(

time: 104 us -> 96.2 us (0.925)
  Pallas kernels: 102 us -> 94.3 us
    pallas_call x1, Pallas kernels: 102 us -> 94.3 us  [shards(): pl.pallas_call(kernel, name='bddc_steps', out_shape=jax.ShapeDtypeStruct(...]
where the time goes in v2:
time: 96.2 us; the launch traced here: 96 us
  Pallas kernels  94.3 us (98%)
  local copies, waits for them, and re-layouts  1.67 us (2%)
    pallas_call x1, Pallas kernels, shards(): pl.pallas_call(kernel, name='bddc_steps', out_shape=jax.ShapeDtypeStruct(...  94.3 us

profile of v2, /device:TPU:1, one launch (start us, length us, event | category | flops | bytes accessed | tf_op | source)
XLA Modules:
  0.0 96.0 jit_solution(2341950975306829301)
XLA Ops:
  0.0 94.3 %bddc_steps.1 = bf16[1024,128]{1,0:T(8,128)(2,1)} custom-call(bf16[1024,1024]{1,0:T(8,128)(2,1)} %bitcast.10, bf16[1024,1024]{1,0:T(8,128)(2,1)} %bitcast.11, f32[8,128]{1,0:T(8,128)} %bitcast.17, bf16[24,1024]{1,0:T(8,128)(2,1)} %bitcast.15, f32[12,1,768]{2,1,0:T(1,128)} %bitcast.16, s32[1,1536]{1,0:T(1,128)} %num_hbm.1, bf16[1024,128]{1,0:T(8,128)(2,1)} %bitcast.13, ...), custom_call_target="tpu_custom_call" | custom-call | tf_op jit(solution)/shard_map/bddc_steps/pallas_call | solution.py:376
  94.4 1.7 %copy.10 = bf16[1,1,1024,128]{3,2,1,0:T(8,128)(2,1)} copy(bf16[1,1,1024,128]{3,2,1,0:T(8,128)(2,1)} %bitcast.12) | data formatting | bytes 524288

commit v3 on v2

--- a/solution.py
+++ b/solution.py
@@ -92,13 +92,23 @@
     def ga_copy(k):
         return rc(ga_src.at[(yc + k) % 8], ga_dst.at[yc], ga_s.at[k], ga_r.at[k], yc_peer(k))
 
-    def gb_copy(k):
-        here = pl.ds(pl.multiple_of(z * 96, 8), 96)
-        return rc(slab1, all1.at[here], gb_s.at[0, k], gb_r.at[0, k], z_peer(k))
-
-    def gc_copy(k):
-        here = pl.ds(pl.multiple_of(z * 48, 8), 48)
-        return rc(slab2, all2.at[here], gb_s.at[1, k], gb_r.at[1, k], z_peer(k))
+    def slab_at(p, rows):
+        return pl.ds(pl.multiple_of(p * rows, 8), rows)
+
+    def gb_copies(i):
+        step = (2, 6, 1, 7, 1, 7)[i]
+        owner = (z + (0, 0, 0, 0, 6, 2)[i]) % 8
+        there = z_peer(step)
+        src1, src2 = (slab1, slab2) if i < 4 else (all1.at[slab_at(owner, 96)], all2.at[slab_at(owner, 48)])
+        return [
+            rc(src1, all1.at[slab_at(owner, 96)], gb_s.at[0, i], gb_r.at[0, i], there),
+            rc(src2, all2.at[slab_at(owner, 48)], gb_s.at[1, i], gb_r.at[1, i], there),
+        ]
+
+    def gc_copy(i):
+        every, rows = ((all1, 96), (all2, 48))[i]
+        here = slab_at((z + (6, 2)[i]) % 8, rows)
+        return rc(every.at[here], every.at[here], gb_s.at[i, 6], gb_r.at[i, 6], z_peer((2, 6)[i]))
 
     load_s, load_n, load_w, load_bt, load_inv, load_num, load_l, load_x = [
         pltpu.make_async_copy(a, b, load_sem.at[i])
@@ -162,13 +172,7 @@
     for f in range(4):
         nb_src[f] = basis[:, f * FACE : (f + 1) * FACE]
 
-    pl.semaphore_wait(barrier, 26)
-    for k in FAR_FIRST:
-        ga_copy(k).start()
     ga_dst[yc] = ga_src[yc]
-    for f in range(4):
-        nb_copy(f).start()
-
     load_w.wait()
     for q in range(8):
         wide = jnp.broadcast_to(w_ref[q : q + 1, :], (128, 128))
@@ -178,11 +182,10 @@
     load_s.wait()
     load_l.wait()
 
-    def send_part(it, current):
-        for f in (1, 0, 3, 2):
+    def make_part(it, current):
+        for f in range(4):
             image = dot(s_ref[face(f), :], current)
             ex_src[it, face(f), :] = l_ref[face(f), :].astype(F32) - image
-            ex_copy(it, f).start()
 
     def make_slabs():
         for k in range(1, 8):
@@ -192,11 +195,19 @@
         slab = jnp.concatenate(low + high, axis=0)
         slab1[...] = slab[:, 0:128]
         slab2[...] = slab[0:48, 128:256] + pltpu.roll(slab[48:96, 128:256], 64, axis=1)
-        for k in FAR_FIRST:
-            gb_copy(k).start()
-            gc_copy(k).start()
+        for i in range(4):
+            for copy in gb_copies(i):
+                copy.start()
         all1[pl.ds(pl.multiple_of(z * 96, 8), 96), :] = slab1[...]
         all2[pl.ds(pl.multiple_of(z * 48, 8), 48), :] = slab2[...]
+
+    def relay_slabs():
+        for i in range(2):
+            for copy in gb_copies(i):
+                copy.wait_recv()
+            for copy in gb_copies(4 + i):
+                copy.start()
+            gc_copy(i).start()
 
     def make_basis():
         for f in range(4):
@@ -235,9 +246,11 @@
             x_now[face(f), :] = (x_fine[face(f), :] + coarse).astype(BF16)
 
     def make_a():
-        for k in range(1, 8):
-            gb_copy(k).wait_recv()
-            gc_copy(k).wait_recv()
+        for i in range(2, 6):
+            for copy in gb_copies(i):
+                copy.wait_recv()
+        for i in range(2):
+            gc_copy(i).wait_recv()
 
         def column(at):
             return jnp.broadcast_to(rows_ref[at : at + 1, :], (128, 256)).T[0:192, :]
@@ -286,6 +299,7 @@
 
         @pl.when(it == 0)
         def _():
+            relay_slabs()
             make_basis()
             make_a()
 
@@ -305,7 +319,7 @@
 
         @pl.when(it + 1 < ITERS)
         def _():
-            send_part(it + 1, x_fine[...].astype(BF16))
+            make_part(it + 1, x_fine[...].astype(BF16))
 
         total = part[it, pl.ds(pl.multiple_of(yc * 24, 8), 24), :]
         for k in range(1, 8):
@@ -319,6 +333,8 @@
         def _():
             for i in (9, 10, 11, 12, 5, 6, 7, 8):
                 ow_copy(it, i).start()
+            for f in (1, 0, 3, 2):
+                ex_copy(it + 1, f).start()
 
             @pl.when(it == 0)
             def _():
@@ -335,7 +351,14 @@
         return carry
 
     x_now = o_ref
-    send_part(0, x_now[...])
+    make_part(0, x_now[...])
+    pl.semaphore_wait(barrier, 26)
+    for k in FAR_FIRST:
+        ga_copy(k).start()
+    for f in (1, 0, 3, 2):
+        ex_copy(0, f).start()
+    for f in range(4):
+        nb_copy(f).start()
     lax.fori_loop(0, ITERS, step, 0)
     for i in range(1, 5):
         ow_copy(ITERS - 1, i).wait_recv()
@@ -363,8 +386,11 @@
         t_copy(f).wait_send()
     for k in range(1, 8):
         ga_copy(k).wait_send()
-        gb_copy(k).wait_send()
-        gc_copy(k).wait_send()
+    for i in range(6):
+        for copy in gb_copies(i):
+            copy.wait_send()
+    for i in range(2):
+        gc_copy(i).wait_send()
 
 
 def shards(schur_t, neumann_t, face_weights, coarse_basis, coarse_inverse, coarse_number, loads, iterate):

time: 96.2 us -> 96.8 us (level)
  no operation moved by 1% of the time
where the time goes in v3:
time: 96.8 us; the launch traced here: 96.7 us
  Pallas kernels  95 us (98%)
  local copies, waits for them, and re-layouts  1.67 us (2%)
    pallas_call x1, Pallas kernels, shards(): pl.pallas_call(kernel, name='bddc_steps', out_shape=jax.ShapeDtypeStruct(...  95 us

profile of v3, /device:TPU:1, one launch (start us, length us, event | category | flops | bytes accessed | tf_op | source)
XLA Modules:
  0.0 96.7 jit_solution(4781454054151061049)
XLA Ops:
  0.0 95.0 %bddc_steps.1 = bf16[1024,128]{1,0:T(8,128)(2,1)} custom-call(bf16[1024,1024]{1,0:T(8,128)(2,1)} %bitcast.10, bf16[1024,1024]{1,0:T(8,128)(2,1)} %bitcast.11, f32[8,128]{1,0:T(8,128)} %bitcast.17, bf16[24,1024]{1,0:T(8,128)(2,1)} %bitcast.15, f32[12,1,768]{2,1,0:T(1,128)} %bitcast.16, s32[1,1536]{1,0:T(1,128)} %num_hbm.1, bf16[1024,128]{1,0:T(8,128)(2,1)} %bitcast.13, ...), custom_call_target="tpu_custom_call" | custom-call | tf_op jit(solution)/shard_map/bddc_steps/pallas_call | solution.py:402
  95.0 1.7 %copy.10 = bf16[1,1,1024,128]{3,2,1,0:T(8,128)(2,1)} copy(bf16[1,1,1024,128]{3,2,1,0:T(8,128)(2,1)} %bitcast.12) | data formatting | bytes 524288

commit v4 on v3

--- a/solution.py
+++ b/solution.py
@@ -60,9 +60,11 @@
     def face(f):
         return pl.ds(f * FACE, FACE)
 
-    def ex_copy(it, f):
+    def ex_copy(it, f, half):
         m = mate[f]
-        return rc(ex_src.at[it, face(f)], ex_dst.at[it, face(m)], ex_s.at[it, f], ex_r.at[it, m], near[f])
+        here, there = pl.ds(f * FACE + half * 128, 128), pl.ds(m * FACE + half * 128, 128)
+        sems = ex_s.at[it, 2 * f + half], ex_r.at[it, 2 * m + half]
+        return rc(ex_src.at[it, here], ex_dst.at[it, there], *sems, near[f])
 
     def up_copy(it, f):
         m = mate[f]
@@ -280,7 +282,8 @@
         mine = pl.ds(pl.multiple_of(z * 24, 8), 24)
         local = jnp.zeros((24, 128), F32)
         for f in (2, 3, 0, 1):
-            ex_copy(it, mate[f]).wait_recv()
+            ex_copy(it, mate[f], 0).wait_recv()
+            ex_copy(it, mate[f], 1).wait_recv()
             resid = ex_src[it, face(f), :] + ex_dst[it, face(f), :] - corr[face(f), :]
             weighted = (wb[face(f), :] * resid).astype(BF16)
             wt[face(f), :] = weighted
@@ -320,6 +323,8 @@
         @pl.when(it + 1 < ITERS)
         def _():
             make_part(it + 1, x_fine[...].astype(BF16))
+            for f in (1, 0, 3, 2):
+                ex_copy(it + 1, f, 0).start()
 
         total = part[it, pl.ds(pl.multiple_of(yc * 24, 8), 24), :]
         for k in range(1, 8):
@@ -334,7 +339,7 @@
             for i in (9, 10, 11, 12, 5, 6, 7, 8):
                 ow_copy(it, i).start()
             for f in (1, 0, 3, 2):
-                ex_copy(it + 1, f).start()
+                ex_copy(it + 1, f, 1).start()
 
             @pl.when(it == 0)
             def _():
@@ -355,10 +360,11 @@
     pl.semaphore_wait(barrier, 26)
     for k in FAR_FIRST:
         ga_copy(k).start()
-    for f in (1, 0, 3, 2):
-        ex_copy(0, f).start()
     for f in range(4):
         nb_copy(f).start()
+    for f in (1, 0, 3, 2):
+        ex_copy(0, f, 0).start()
+        ex_copy(0, f, 1).start()
     lax.fori_loop(0, ITERS, step, 0)
     for i in range(1, 5):
         ow_copy(ITERS - 1, i).wait_recv()
@@ -366,7 +372,8 @@
 
     def drain(it, carry):
         for f in range(4):
-            ex_copy(it, f).wait_send()
+            ex_copy(it, f, 0).wait_send()
+            ex_copy(it, f, 1).wait_send()
             up_copy(it, f).wait_send()
             ow_copy(it, f + 1).wait_send()
         for k in range(1, 8):
@@ -446,7 +453,7 @@
             pltpu.VMEM((4, 24, 256), F32),
             pltpu.VMEM((4, 24, 256), F32),
             dma((8,)),
-            dma((ITERS, 4)), dma((ITERS, 4)),
+            dma((ITERS, 8)), dma((ITERS, 8)),
             dma((ITERS, 4)), dma((ITERS, 4)),
             dma((ITERS, 8)), dma((ITERS, 8)),
             dma((ITERS, 8)), dma((ITERS, 8)),

time: 96.8 us -> 94.5 us (0.976)
  Pallas kernels: 95 us -> 92.7 us
    pallas_call x1, Pallas kernels: 95 us -> 92.7 us  [shards(): pl.pallas_call(kernel, name='bddc_steps', out_shape=jax.ShapeDtypeStruct(...]
where the time goes in v4:
time: 94.5 us; the launch traced here: 94.4 us
  Pallas kernels  92.7 us (98%)
  local copies, waits for them, and re-layouts  1.67 us (2%)
    pallas_call x1, Pallas kernels, shards(): pl.pallas_call(kernel, name='bddc_steps', out_shape=jax.ShapeDtypeStruct(...  92.7 us

profile of v4, /device:TPU:1, one launch (start us, length us, event | category | flops | bytes accessed | tf_op | source)
XLA Modules:
  0.0 94.4 jit_solution(17507436418435759077)
XLA Ops:
  0.0 92.7 %bddc_steps.1 = bf16[1024,128]{1,0:T(8,128)(2,1)} custom-call(bf16[1024,1024]{1,0:T(8,128)(2,1)} %bitcast.10, bf16[1024,1024]{1,0:T(8,128)(2,1)} %bitcast.11, f32[8,128]{1,0:T(8,128)} %bitcast.17, bf16[24,1024]{1,0:T(8,128)(2,1)} %bitcast.15, f32[12,1,768]{2,1,0:T(1,128)} %bitcast.16, s32[1,1536]{1,0:T(1,128)} %num_hbm.1, bf16[1024,128]{1,0:T(8,128)(2,1)} %bitcast.13, ...), custom_call_target="tpu_custom_call" | custom-call | tf_op jit(solution)/shard_map/bddc_steps/pallas_call | solution.py:409
  92.7 1.7 %copy.10 = bf16[1,1,1024,128]{3,2,1,0:T(8,128)(2,1)} copy(bf16[1,1,1024,128]{3,2,1,0:T(8,128)(2,1)} %bitcast.12) | data formatting | bytes 524288

commit v5 on v4

--- a/solution.py
+++ b/solution.py
@@ -119,10 +119,9 @@
              (num_hbm, num_ref), (l_hbm, l_ref), (x_hbm, o_ref)]
         )
     ]
-    for load in (load_num, load_inv, load_bt, load_w, load_x, load_s, load_l, load_n):
+    for load in (load_num, load_inv, load_x, load_s, load_l, load_bt, load_w, load_n):
         load.start()
-    c_all[...] = jnp.zeros_like(c_all)
-    corr[...] = jnp.zeros_like(corr)
+    c_all[:, 192:256, :] = jnp.zeros((ITERS, 64, 128), F32)
 
     barrier = pltpu.get_barrier_semaphore()
     for dev in around + [z_peer(k) for k in range(1, 8)] + [yc_peer(k) for k in range(1, 8)]:
@@ -143,14 +142,6 @@
         here = (lane >= 24 * p) & (lane < 24 * p + 24)
         cols = jnp.where(here, pltpu.roll(turns[p], 24 * p, axis=1), cols)
     cols_ref[...] = cols
-    n = planes[pl.ds(z, 1), :]
-    zn = (n * 683) >> 16
-    dn = (n * 5462) >> 16
-    i, dn = n - 12 * dn, dn - 8 * zn
-    r = jnp.where(i < 8, dn * 8 + i, 56 + dn * 4 + i)
-    rows_ref[0:1, :] = zn * 96 + r
-    rows_ref[1:2, :] = jnp.where(r < 48, zn * 48 + r, -1)
-    rows_ref[2:3, :] = jnp.where(r >= 48, zn * 48 + r - 48, -1)
 
     load_inv.wait()
     inv16[...] = jnp.zeros_like(inv16)
@@ -175,15 +166,6 @@
         nb_src[f] = basis[:, f * FACE : (f + 1) * FACE]
 
     ga_dst[yc] = ga_src[yc]
-    load_w.wait()
-    for q in range(8):
-        wide = jnp.broadcast_to(w_ref[q : q + 1, :], (128, 128))
-        wb[q * 128 : (q + 1) * 128, :] = wide.T
-
-    load_x.wait()
-    load_s.wait()
-    load_l.wait()
-
     def make_part(it, current):
         for f in range(4):
             image = dot(s_ref[face(f), :], current)
@@ -356,15 +338,31 @@
         return carry
 
     x_now = o_ref
-    make_part(0, x_now[...])
     pl.semaphore_wait(barrier, 26)
     for k in FAR_FIRST:
         ga_copy(k).start()
     for f in range(4):
         nb_copy(f).start()
+    load_x.wait()
+    load_s.wait()
+    load_l.wait()
+    make_part(0, x_now[...])
     for f in (1, 0, 3, 2):
         ex_copy(0, f, 0).start()
         ex_copy(0, f, 1).start()
+    n = planes[pl.ds(z, 1), :]
+    zn = (n * 683) >> 16
+    dn = (n * 5462) >> 16
+    i, dn = n - 12 * dn, dn - 8 * zn
+    r = jnp.where(i < 8, dn * 8 + i, 56 + dn * 4 + i)
+    rows_ref[0:1, :] = zn * 96 + r
+    rows_ref[1:2, :] = jnp.where(r < 48, zn * 48 + r, -1)
+    rows_ref[2:3, :] = jnp.where(r >= 48, zn * 48 + r - 48, -1)
+    load_w.wait()
+    for q in range(8):
+        wide = jnp.broadcast_to(w_ref[q : q + 1, :], (128, 128))
+        wb[q * 128 : (q + 1) * 128, :] = wide.T
+    corr[...] = jnp.zeros_like(corr)
     lax.fori_loop(0, ITERS, step, 0)
     for i in range(1, 5):
         ow_copy(ITERS - 1, i).wait_recv()
@@ -464,7 +462,7 @@
             dma((4,)), dma((4,)),
         ],
         compiler_params=pltpu.CompilerParams(
-            collective_id=0, has_side_effects=True, vmem_limit_bytes=67000000
+            collective_id=0, has_side_effects=True, vmem_limit_bytes=66700000
         ),
     )(schur_t[0, 0], neumann_t[0, 0], weights, basis_t, coarse_inverse.reshape(12, 1, 768), coarse_number, loads[0, 0], iterate[0, 0])
     return out[None, None]

time: 94.5 us -> 95 us (level)
  no operation moved by 1% of the time
where the time goes in v5:
time: 95 us; the launch traced here: 94.8 us
  Pallas kernels  93.2 us (98%)
  local copies, waits for them, and re-layouts  1.67 us (2%)
    pallas_call x1, Pallas kernels, shards(): pl.pallas_call(kernel, name='bddc_steps', out_shape=jax.ShapeDtypeStruct(...  93.2 us

profile of v5, /device:TPU:1, one launch (start us, length us, event | category | flops | bytes accessed | tf_op | source)
XLA Modules:
  0.0 94.8 jit_solution(3921425359143227847)
XLA Ops:
  0.0 93.2 %bddc_steps.1 = bf16[1024,128]{1,0:T(8,128)(2,1)} custom-call(bf16[1024,1024]{1,0:T(8,128)(2,1)} %bitcast.10, bf16[1024,1024]{1,0:T(8,128)(2,1)} %bitcast.11, f32[8,128]{1,0:T(8,128)} %bitcast.17, bf16[24,1024]{1,0:T(8,128)(2,1)} %bitcast.15, f32[12,1,768]{2,1,0:T(1,128)} %bitcast.16, s32[1,1536]{1,0:T(1,128)} %num_hbm.1, bf16[1024,128]{1,0:T(8,128)(2,1)} %bitcast.13, ...), custom_call_target="tpu_custom_call" | custom-call | tf_op jit(solution)/shard_map/bddc_steps/pallas_call | solution.py:407
  93.2 1.7 %copy.10 = bf16[1,1,1024,128]{3,2,1,0:T(8,128)(2,1)} copy(bf16[1,1,1024,128]{3,2,1,0:T(8,128)(2,1)} %bitcast.12) | data formatting | bytes 524288
